TPU v7x, 32 devices: a whole 2x2x4 slice. The times are simulated.
32 devices in a mesh: island: 8 (over z, x), fsdp: 4 (over y, core).
Axes of the slice: x: 2, y: 2, z: 4, core: 2. Of those that a mesh axis runs over, the one named last changes fastest.
Arguments:
- local_weights: bfloat16 [8, 4096, 512], P('island', 'fsdp'), may hold values from -6 to 6
- adam_first: bfloat16 [8, 4096, 512], P('island', 'fsdp'), may hold values from -6 to 6
- adam_second: bfloat16 [8, 4096, 512], P('island', 'fsdp'), may hold values from 0.5 to 4
- global_weights: float32 [4096, 512], P('fsdp'), may hold values from -6 to 6
- outer_momentum: float32 [4096, 512], P('fsdp'), may hold values from -3 to 3
- inputs: bfloat16 [8, 512, 4096], P('island', 'fsdp'), may hold values from -6 to 6
- key_cotangent: bfloat16 [8, 512, 512], P('island', 'fsdp'), may hold values from -24 to 24
Outputs:
- new_local: bfloat16 [8, 4096, 512], P('island', 'fsdp')
- new_first: bfloat16 [8, 4096, 512], P('island', 'fsdp')
- new_second: bfloat16 [8, 4096, 512], P('island', 'fsdp')
- new_global: float32 [4096, 512], P('fsdp')
- new_momentum: float32 [4096, 512], P('fsdp')
All inputs are finite; a program needn't handle non-finite values.
Results may differ from a plain program's by a relative error of at most 0.0065.
Values may be sent and summed in bfloat16 or wider, within the bound.
A program may use at most 64 MiB of HBM per device.

v0:
```python
import jax
import jax.numpy as jnp
from jax import lax
from jax.sharding import PartitionSpec as P

HEAD_DIM = 128
beta_one = 0.9
beta_two = 0.95
inner_rate = 0.02
weight_decay = 0.1
adam_epsilon = 1e-08
norm_epsilon = 1e-06
outer_rate = 0.7
outer_beta = 0.9
merge_weight = 0.5


def key_backward(keys, upstream):
    heads = keys.shape[1] // HEAD_DIM
    shaped = keys.reshape(keys.shape[0], heads, HEAD_DIM)
    cotan_heads = upstream.reshape(keys.shape[0], heads, HEAD_DIM)
    squares = jnp.mean(shaped * shaped, axis=-1, keepdims=True)
    inverse = lax.rsqrt(squares + norm_epsilon)
    normed = shaped * inverse
    projected = jnp.mean(cotan_heads * normed, axis=-1, keepdims=True)
    return (inverse * (cotan_heads - normed * projected)).reshape(keys.shape)


def local(
    local_weights, adam_first, adam_second, global_weights, outer_momentum, inputs, key_cotangent
):
    weights = local_weights[0]
    tokens = inputs[0]
    upstream = key_cotangent[0].astype(jnp.float32)
    scale = float(tokens.shape[1]) ** (-0.5)
    islands = lax.axis_size("island")
    summed = lax.psum(weights.astype(jnp.float32), "island")
    outer_grad = global_weights - summed / islands
    new_momentum = outer_beta * outer_momentum + outer_grad
    new_global = global_weights - outer_rate * (outer_grad + outer_beta * new_momentum)
    columns = tokens
    keys = (
        jnp.dot(
            columns,
            lax.all_gather(weights, "fsdp", axis=0, tiled=True),
            preferred_element_type=jnp.float32,
        )
        * scale
    )
    key_grad = (key_backward(keys, upstream) * scale).astype(jnp.bfloat16)
    columns = tokens
    gradient = lax.psum_scatter(
        lax.dot_general(
            columns, key_grad, (((0,), (0,)), ((), ())), preferred_element_type=jnp.float32
        ).astype(jnp.bfloat16),
        "fsdp",
        scatter_dimension=0,
        tiled=True,
    ).astype(jnp.float32)
    first_new = beta_one * adam_first[0].astype(jnp.float32) + (1.0 - beta_one) * gradient
    second_new = (
        beta_two * adam_second[0].astype(jnp.float32) + (1.0 - beta_two) * gradient * gradient
    )
    current = weights.astype(jnp.float32)
    inner = current - inner_rate * (
        first_new / (jnp.sqrt(second_new) + adam_epsilon) + weight_decay * current
    )
    merged = merge_weight * inner + (1.0 - merge_weight) * new_global
    return (
        merged.astype(jnp.bfloat16)[None],
        first_new.astype(jnp.bfloat16)[None],
        second_new.astype(jnp.bfloat16)[None],
        new_global,
        new_momentum,
    )


def solution(mesh):
    placed = (
        P("island", "fsdp", None),
        P("island", "fsdp", None),
        P("island", "fsdp", None),
        P("fsdp", None),
        P("fsdp", None),
        P("island", "fsdp", None),
        P("island", "fsdp", None),
    )
    return jax.shard_map(
        local,
        mesh=mesh,
        in_specs=placed,
        out_specs=(
            P("island", "fsdp", None),
            P("island", "fsdp", None),
            P("island", "fsdp", None),
            P("fsdp", None),
            P("fsdp", None),
        ),
        check_vma=False,
    )
```

profile of v0, /device:TPU:0, one launch (start us, length us, event | category | flops | bytes accessed | tf_op | source)
XLA Modules:
  0.0 142.2 jit_solution(9254017359627056663)
XLA Ops:
  8.0 0.0 copy-start
  8.0 0.0 all-gather.3.cloned.1.call-start
  8.1 0.7 all-gather.3.cloned.1.call-update
  8.7 0.0 all-reduce.2.cloned.1.call-start
  8.8 1.5 %copy.12 = bf16[1,1024,512]{1,2,0:T(8,128)(2,1)S(1)} copy(bf16[1,1024,512]{2,1,0:T(8,128)(2,1)} %param.7) | data formatting | bytes 2097152 | tf_op args[0]
  10.3 0.0 copy-start.3
  10.3 1.6 %bitcast_convert_fusion = f32[1024,512]{0,1:T(8,128)} fusion(bf16[1,1024,512]{1,2,0:T(8,128)(2,1)S(1)} %copy.12), kind=kLoop, calls=%fused_computation.17 | loop fusion | flops 524288 | bytes 3145728 | tf_op jit(solution)/shard_map/convert_element_type | solution.py:64
  11.9 0.0 all-reduce.2.cloned.1.call-update
  11.9 0.0 reduce-scatter.2.cloned.1.call-start
  12.0 0.0 copy-done.3
  12.0 0.1 reshape.52
  12.1 35.5 %all-gather.3.cloned.1.call-done = bf16[1,4096,512]{2,1,0:T(8,128)(2,1)} async-done(((bf16[1,1024,512]{2,1,0:T(8,128)(2,1)}), bf16[1,4096,512]{2,1,0:T(8,128)(2,1)}) %all-gather.3.cloned.1.call-update) | async-done | bytes 4194320 | tf_op jit(solution)/shard_map/all_gather | solution.py:45
  47.6 0.0 copy-done
  47.6 2.9 %fusion.7 = f32[128,512]{1,0:T(8,128)S(1)} fusion(bf16[1,4096,512]{2,1,0:T(8,128)(2,1)} %all-gather.3.cloned.1.call-done, bf16[1,128,4096]{2,1,0:T(8,128)(2,1)S(1)} %copy-done), kind=kOutput, calls=%fused_computation.14 | convolution fusion | flops 536936448 | bytes 5505024 | tf_op jit(solution)/shard_map/dot_general | solution.py:43
  50.5 0.1 reshape.50
  50.6 0.2 multiply_reduce_fusion.1
  50.8 0.4 multiply_reduce_fusion
  51.2 0.2 mul.112
  51.4 0.2 mul.107
  51.6 3.3 %fusion = bf16[4096,512]{0,1:T(8,128)(2,1)} fusion(bf16[1,128,4096]{2,1,0:T(8,128)(2,1)S(1)} %copy-done, f32[16,8,4,128]{3,2,1,0:T(4,128)S(1)} %bitcast.65, f32[128,512]{1,0:T(8,128)S(1)} %fusion.7, f32[16,8,4,128]{3,2,1,0:T(4,128)S(1)} %bitcast.66, bf16[1,128,512]{2,1,0:T(8,128)(2,1)S(1)} %copy-done.3), kind=kOutput, calls=%fused_computation.1 | convolution fusion | flops 539426816 | bytes 6160384 | tf_op jit(solution)/shard_map/dot_general | solution.py:53
  54.9 0.0 reduce-scatter.2.cloned.1.call-update
  54.9 2.9 %copy.16 = f32[1024,512]{0,1:T(8,128)} copy(f32[1024,512]{1,0:T(8,128)} %param.11) | data formatting | bytes 4194304 | tf_op args[4]
  57.8 2.9 %copy.17 = f32[1024,512]{0,1:T(8,128)} copy(f32[1024,512]{1,0:T(8,128)} %param.10) | data formatting | bytes 4194304 | tf_op args[3]
  60.7 1.5 %copy.13 = bf16[1,1024,512]{1,2,0:T(8,128)(2,1)S(1)} copy(bf16[1,1024,512]{2,1,0:T(8,128)(2,1)} %param.8) | data formatting | bytes 2097152 | tf_op args[1]
  62.3 2.5 %copy.14 = bf16[1,1024,512]{1,2,0:T(8,128)(2,1)} copy(bf16[1,1024,512]{2,1,0:T(8,128)(2,1)} %param.9) | data formatting | bytes 2097152 | tf_op args[2]
  64.8 52.7 %all-reduce.2.cloned.1.call-done = f32[1024,512]{0,1:T(8,128)} async-done(((f32[1024,512]{0,1:T(8,128)}), f32[1024,512]{0,1:T(8,128)}) %all-reduce.2.cloned.1.call-update) | async-done | bytes 2097168 | tf_op jit(solution)/shard_map/psum | solution.py:37
  117.5 0.0 reduce-scatter.2.cloned.1.call-done
  117.5 6.4 %fusion.14 = (bf16[1,1024,512]{1,2,0:T(8,128)(2,1)}, f32[1024,512]{0,1:T(8,128)}, f32[1024,512]{0,1:T(8,128)}, bf16[1,1024,512]{1,2,0:T(8,128)(2,1)}, bf16[1,1024,512]{1,2,0:T(8,128)(2,1)}) fusion(bf16[1,1024,512]{1,2,0:T(8,128)(2,1)} %copy.14, bf16[1024,512]{0,1:T(8,128)(2,1)} %reduce-scatter.2.cloned.1.call-done, bf16[1,1024,512]{1,2,0:T(8,128)(2,1)S(1)} %copy.13, ...), kind=kLoop, calls=%fused_computation.20 | loop fusion | flops 15728640 | bytes 17825792 | tf_op jit(solution)/shard_map/broadcast_in_dim | solution.py:70
  123.9 2.9 %copy.21 = f32[1024,512]{1,0:T(8,128)} copy(f32[1024,512]{0,1:T(8,128)} %get-tuple-element.11) | data formatting | bytes 4194304
  126.8 2.9 %copy.22 = f32[1024,512]{1,0:T(8,128)} copy(f32[1024,512]{0,1:T(8,128)} %get-tuple-element.12) | data formatting | bytes 4194304
  129.7 0.0 copy-start.2
  129.7 0.0 copy-start.1
  129.7 2.4 %copy.18 = bf16[1,1024,512]{2,1,0:T(8,128)(2,1)} copy(bf16[1,1024,512]{1,2,0:T(8,128)(2,1)} %get-tuple-element.10) | data formatting | bytes 2097152
  132.1 0.0 copy-done.2
  132.1 1.3 copy.19
  133.4 0.0 copy-done.1
  133.4 1.3 copy.20
  (2 shorter events, 0.0 us)
Async XLA Ops:
  8.0 39.6 %copy-start = (bf16[1,128,4096]{2,1,0:T(8,128)(2,1)S(1)}, bf16[1,128,4096]{2,1,0:T(8,128)(2,1)}, u32[]{:S(2)}) copy-start(bf16[1,128,4096]{2,1,0:T(8,128)(2,1)} %param.12) | copy-start | bytes 3145732
  8.0 39.6 %all-gather.3.cloned.1.call-start = ((), (), s32[]{:S(2)}) async-start(), calls=%async_computation.3 | async-start | bytes 5242880 | tf_op jit(solution)/shard_map/all_gather | solution.py:45
  8.7 108.8 %all-reduce.2.cloned.1.call-start = ((), (), s32[]{:S(2)}) async-start(), calls=%async_computation.2 | async-start | bytes 4194304 | tf_op jit(solution)/shard_map/psum | solution.py:37
  10.3 1.7 %copy-start.3 = (bf16[1,128,512]{2,1,0:T(8,128)(2,1)S(1)}, bf16[1,128,512]{2,1,0:T(8,128)(2,1)}, u32[]{:S(2)}) copy-start(bf16[1,128,512]{2,1,0:T(8,128)(2,1)} %param.13) | copy-start | bytes 393220
  11.9 105.6 %reduce-scatter.2.cloned.1.call-start = ((), (), s32[]{:S(2)}) async-start(), calls=%async_computation.1 | async-start | bytes 5242880 | tf_op jit(solution)/shard_map/reduce_scatter | solution.py:52
  129.7 2.4 %copy-start.2 = (bf16[1,1024,512]{1,2,0:T(8,128)(2,1)S(1)}, bf16[1,1024,512]{1,2,0:T(8,128)(2,1)}, u32[]{:S(2)}) copy-start(bf16[1,1024,512]{1,2,0:T(8,128)(2,1)} %get-tuple-element.14) | copy-start | bytes 3145732
  129.7 3.7 %copy-start.1 = (bf16[1,1024,512]{1,2,0:T(8,128)(2,1)S(1)}, bf16[1,1024,512]{1,2,0:T(8,128)(2,1)}, u32[]{:S(2)}) copy-start(bf16[1,1024,512]{1,2,0:T(8,128)(2,1)} %get-tuple-element.13) | copy-start | bytes 3145732
Sparse Core Ops, SparseCore 0:
  10.4 37.1 all-gather.2
  55.0 44.4 reduce-scatter.1
Sparse Core Ops, SparseCore 1:
  12.8 104.6 all-reduce.1
where the time goes:
time: 143 us; the launch traced here: 142 us
  waiting for transfers between devices  88.9 us (62%)
  local copies, waits for them, and re-layouts  22.8 us (16%)
  between operations  15.6 us (11%)
  other arithmetic  8.62 us (6%)
  matrix products  6.16 us (4%)
    psum x1, waiting for transfers between devices, local(): summed = lax.psum(weights.astype(jnp.float32), 'island')  52.7 us
    all_gather x1, waiting for transfers between devices, local(): lax.all_gather(weights, 'fsdp', axis=0, tiled=True)  35.5 us
    unnamed x18, local copies, waits for them, and re-layouts  22.2 us
    broadcast_in_dim x1, other arithmetic, local(): merged.astype(jnp.bfloat16)[None]  6.43 us
    dot_general x1, matrix products, local(): lax.dot_general(columns, key_grad, (((0,), (0,)), ((), ())), preferred_el...  3.25 us
    dot_general x1, matrix products, local(): jnp.dot(columns, lax.all_gather(weights, 'fsdp', axis=0, tiled=True), pre...  2.9 us
  transfers between devices with their start and end apart: 3, of which 2 were waited for; matrix products, arithmetic and copies ran while one was open for 14% of the time, Pallas kernels for 0%

commit v1 on v0

--- a/solution.py
+++ b/solution.py
@@ -42,7 +42,9 @@
     keys = (
         jnp.dot(
             columns,
-            lax.all_gather(weights, "fsdp", axis=0, tiled=True),
+            jnp.concatenate(
+                lax.all_to_all(jnp.stack([weights] * lax.axis_size("fsdp")), "fsdp", 0, 0), axis=0
+            ),
             preferred_element_type=jnp.float32,
         )
         * scale

time: 143 us -> 152 us (1.063)
  starting transfers between devices: 0.12 us -> 5.06 us
  local copies, waits for them, and re-layouts: 22.8 us -> 25.4 us
  waiting for transfers between devices: 88.9 us -> 90.5 us
    all_to_all x0 -> x1, waiting for transfers between devices: none -> 46.6 us  [local(): lax.all_to_all(jnp.stack([weights] * lax.axis_size('fsdp')), 'fsdp', 0, 0)]
    all_gather x1 -> x0, waiting for transfers between devices: 35.5 us -> none  [local(): lax.all_gather(weights, 'fsdp', axis=0, tiled=True)]
    psum x1, waiting for transfers between devices: 52.7 us -> 43.9 us  [local(): summed = lax.psum(weights.astype(jnp.float32), 'island')]
    all_to_all x0 -> x1, starting transfers between devices: none -> 4.97 us  [local(): lax.all_to_all(jnp.stack([weights] * lax.axis_size('fsdp')), 'fsdp', 0, 0)]
    another operation x0 -> x1, local copies, waits for them, and re-layouts: none -> 3.62 us  [local(): jnp.stack([weights] * lax.axis_size('fsdp'))]
    unnamed x18 -> x20, local copies, waits for them, and re-layouts: 22.2 us -> 21.2 us
  transfers between devices with their start and end apart: 3 -> 3, of which waited for: 2 -> 2; matrix products, arithmetic and copies ran while one was open for 14% -> 13% of each run, Pallas kernels for 0% -> 0%
where the time goes in v1:
time: 152 us; the launch traced here: 151 us
  waiting for transfers between devices  90.5 us (60%)
  local copies, waits for them, and re-layouts  25.4 us (17%)
  between operations  15.6 us (10%)
  other arithmetic  8.57 us (6%)
  matrix products  6.18 us (4%)
  starting transfers between devices  5.06 us (3%)
    all_to_all x1, waiting for transfers between devices, local(): lax.all_to_all(jnp.stack([weights] * lax.axis_size('fsdp')), 'fsdp', 0, 0)  46.6 us
    psum x1, waiting for transfers between devices, local(): summed = lax.psum(weights.astype(jnp.float32), 'island')  43.9 us
    unnamed x20, local copies, waits for them, and re-layouts  21.2 us
    broadcast_in_dim x1, other arithmetic, local(): merged.astype(jnp.bfloat16)[None]  6.43 us
    all_to_all x1, starting transfers between devices, local(): lax.all_to_all(jnp.stack([weights] * lax.axis_size('fsdp')), 'fsdp', 0, 0)  4.97 us
    another operation x1, local copies, waits for them, and re-layouts, local(): jnp.stack([weights] * lax.axis_size('fsdp'))  3.62 us
    dot_general x1, matrix products, local(): lax.dot_general(columns, key_grad, (((0,), (0,)), ((), ())), preferred_el...  3.25 us
  transfers between devices with their start and end apart: 3, of which 2 were waited for; matrix products, arithmetic and copies ran while one was open for 13% of the time, Pallas kernels for 0%

profile of v1, /device:TPU:0, one launch (start us, length us, event | category | flops | bytes accessed | tf_op | source)
XLA Modules:
  0.0 151.3 jit_solution(3507645118649123327)
XLA Ops:
  8.0 0.0 copy-start
  8.0 3.6 %stack.3 = bf16[4,1024,512]{2,1,0:T(8,128)(2,1)} broadcast(bf16[1024,512]{1,0:T(8,128)(2,1)} %bitcast.62), dimensions={1,2} | broadcast | bytes 5242880 | tf_op jit(solution)/shard_map/stack | solution.py:46
  11.6 0.0 copy-start.1
  11.6 5.0 %all-to-all-start = ((bf16[4,1024,512]{2,1,0:T(8,128)(2,1)}), bf16[4,1024,512]{2,1,0:T(8,128)(2,1)}, u32[]{:S(2)}, u32[]{:S(2)}) async-start(bf16[4,1024,512]{2,1,0:T(8,128)(2,1)} %stack.3), calls=%async_computation | async-start | bytes 8388608 | tf_op jit(solution)/shard_map/all_to_all | solution.py:46
  16.6 0.0 all-reduce.2.cloned.1.call-start
  16.7 0.0 copy-done.1
  16.7 0.5 copy.12
  17.2 0.0 copy-start.4
  17.2 1.5 %bitcast_convert_fusion = f32[1024,512]{0,1:T(8,128)} fusion(bf16[1,1024,512]{1,2,0:T(8,128)(2,1)S(1)} %copy.12), kind=kLoop, calls=%fused_computation.17 | loop fusion | flops 524288 | bytes 3145728 | tf_op jit(solution)/shard_map/convert_element_type | solution.py:66
  18.8 0.0 all-reduce.2.cloned.1.call-update
  18.8 0.0 reduce-scatter.2.cloned.1.call-start
  18.8 0.0 copy-done.4
  18.9 0.1 reshape.57
  18.9 46.6 %all-to-all-done = bf16[4,1024,512]{2,1,0:T(8,128)(2,1)} async-done(((bf16[4,1024,512]{2,1,0:T(8,128)(2,1)}), bf16[4,1024,512]{2,1,0:T(8,128)(2,1)}, u32[]{:S(2)}, u32[]{:S(2)}) %all-to-all-start) | async-done | bytes 4194336 | tf_op jit(solution)/shard_map/all_to_all | solution.py:46
  65.5 0.0 copy-done
  65.5 2.9 %convolution_multiply_fusion = f32[128,512]{1,0:T(8,128)S(1)} fusion(bf16[4096,512]{1,0:T(8,128)(2,1)} %bitcast.4, bf16[1,128,4096]{2,1,0:T(8,128)(2,1)S(1)} %copy-done), kind=kOutput, calls=%fused_computation.12 | convolution fusion | flops 536936448 | bytes 5505024 | tf_op jit(solution)/shard_map/dot_general | solution.py:43
  68.4 0.1 reshape.55
  68.5 0.2 multiply_reduce_fusion.1
  68.8 0.4 multiply_reduce_fusion
  69.2 0.2 mul.112
  69.4 0.2 mul.107
  69.6 3.3 %fusion = bf16[4096,512]{0,1:T(8,128)(2,1)} fusion(bf16[1,128,4096]{2,1,0:T(8,128)(2,1)S(1)} %copy-done, f32[16,8,4,128]{3,2,1,0:T(4,128)S(1)} %bitcast.63, f32[128,512]{1,0:T(8,128)S(1)} %convolution_multiply_fusion, f32[16,8,4,128]{3,2,1,0:T(4,128)S(1)} %bitcast.64, bf16[1,128,512]{2,1,0:T(8,128)(2,1)S(1)} %copy-done.4), kind=kOutput, calls=%fused_computation.1 | convolution fusion | flops 539426816 | bytes 6160384 | tf_op jit(solution)/shard_map/dot_general | solution.py:55
  72.8 0.0 reduce-scatter.2.cloned.1.call-update
  72.8 2.9 %copy.17 = f32[1024,512]{0,1:T(8,128)} copy(f32[1024,512]{1,0:T(8,128)} %param.11) | data formatting | bytes 4194304 | tf_op args[4]
  75.7 2.9 %copy.18 = f32[1024,512]{0,1:T(8,128)} copy(f32[1024,512]{1,0:T(8,128)} %param.10) | data formatting | bytes 4194304 | tf_op args[3]
  78.6 1.7 %copy.13 = bf16[1,1024,512]{1,2,0:T(8,128)(2,1)S(1)} copy(bf16[1,1024,512]{2,1,0:T(8,128)(2,1)} %param.8) | data formatting | bytes 2097152 | tf_op args[1]
  80.4 2.3 %copy.15 = bf16[1,1024,512]{1,2,0:T(8,128)(2,1)} copy(bf16[1,1024,512]{2,1,0:T(8,128)(2,1)} %param.9) | data formatting | bytes 2097152 | tf_op args[2]
  82.6 43.9 %all-reduce.2.cloned.1.call-done = f32[1024,512]{0,1:T(8,128)} async-done(((f32[1024,512]{0,1:T(8,128)}), f32[1024,512]{0,1:T(8,128)}) %all-reduce.2.cloned.1.call-update) | async-done | bytes 2097168 | tf_op jit(solution)/shard_map/psum | solution.py:37
  126.6 0.0 reduce-scatter.2.cloned.1.call-done
  126.6 6.4 %fusion.9 = (bf16[1,1024,512]{1,2,0:T(8,128)(2,1)}, f32[1024,512]{0,1:T(8,128)}, f32[1024,512]{0,1:T(8,128)}, bf16[1,1024,512]{1,2,0:T(8,128)(2,1)}, bf16[1,1024,512]{1,2,0:T(8,128)(2,1)}) fusion(bf16[1,1024,512]{1,2,0:T(8,128)(2,1)} %copy.15, bf16[1024,512]{0,1:T(8,128)(2,1)} %reduce-scatter.2.cloned.1.call-done, bf16[1,1024,512]{1,2,0:T(8,128)(2,1)S(1)} %copy.13, ...), kind=kLoop, calls=%fused_computation.18 | loop fusion | flops 15728640 | bytes 17825792 | tf_op jit(solution)/shard_map/broadcast_in_dim | solution.py:72
  133.0 2.9 %copy.22 = f32[1024,512]{1,0:T(8,128)} copy(f32[1024,512]{0,1:T(8,128)} %get-tuple-element.11) | data formatting | bytes 4194304
  135.9 2.9 %copy.23 = f32[1024,512]{1,0:T(8,128)} copy(f32[1024,512]{0,1:T(8,128)} %get-tuple-element.12) | data formatting | bytes 4194304
  138.8 0.0 copy-start.3
  138.8 0.0 copy-start.2
  138.8 2.4 %copy.19 = bf16[1,1024,512]{2,1,0:T(8,128)(2,1)} copy(bf16[1,1024,512]{1,2,0:T(8,128)(2,1)} %get-tuple-element.10) | data formatting | bytes 2097152
  141.2 0.0 copy-done.3
  141.2 1.3 copy.20
  142.5 0.0 copy-done.2
  142.5 1.3 copy.21
  (2 shorter events, 0.0 us)
Async XLA Ops:
  8.0 57.5 %copy-start = (bf16[1,128,4096]{2,1,0:T(8,128)(2,1)S(1)}, bf16[1,128,4096]{2,1,0:T(8,128)(2,1)}, u32[]{:S(2)}) copy-start(bf16[1,128,4096]{2,1,0:T(8,128)(2,1)} %param.12) | copy-start | bytes 3145732
  11.6 5.0 %copy-start.1 = (bf16[1,1024,512]{2,1,0:T(8,128)(2,1)S(1)}, bf16[1,1024,512]{2,1,0:T(8,128)(2,1)}, u32[]{:S(2)}) copy-start(bf16[1,1024,512]{2,1,0:T(8,128)(2,1)} %param.7) | copy-start | bytes 3145732
  11.6 53.9 %all-to-all-start = ((bf16[4,1024,512]{2,1,0:T(8,128)(2,1)}), bf16[4,1024,512]{2,1,0:T(8,128)(2,1)}, u32[]{:S(2)}, u32[]{:S(2)}) async-start(bf16[4,1024,512]{2,1,0:T(8,128)(2,1)} %stack.3), calls=%async_computation | async-start | bytes 8388608 | tf_op jit(solution)/shard_map/all_to_all | solution.py:46
  16.6 110.0 %all-reduce.2.cloned.1.call-start = ((), (), s32[]{:S(2)}) async-start(), calls=%async_computation.3 | async-start | bytes 4194304 | tf_op jit(solution)/shard_map/psum | solution.py:37
  17.2 1.6 %copy-start.4 = (bf16[1,128,512]{2,1,0:T(8,128)(2,1)S(1)}, bf16[1,128,512]{2,1,0:T(8,128)(2,1)}, u32[]{:S(2)}) copy-start(bf16[1,128,512]{2,1,0:T(8,128)(2,1)} %param.13) | copy-start | bytes 393220
  18.8 107.8 %reduce-scatter.2.cloned.1.call-start = ((), (), s32[]{:S(2)}) async-start(), calls=%async_computation.2 | async-start | bytes 5242880 | tf_op jit(solution)/shard_map/reduce_scatter | solution.py:54
  138.8 2.4 %copy-start.3 = (bf16[1,1024,512]{1,2,0:T(8,128)(2,1)S(1)}, bf16[1,1024,512]{1,2,0:T(8,128)(2,1)}, u32[]{:S(2)}) copy-start(bf16[1,1024,512]{1,2,0:T(8,128)(2,1)} %get-tuple-element.14) | copy-start | bytes 3145732
  138.8 3.7 %copy-start.2 = (bf16[1,1024,512]{1,2,0:T(8,128)(2,1)S(1)}, bf16[1,1024,512]{1,2,0:T(8,128)(2,1)}, u32[]{:S(2)}) copy-start(bf16[1,1024,512]{1,2,0:T(8,128)(2,1)} %get-tuple-element.13) | copy-start | bytes 3145732
Sparse Core Ops, SparseCore 0:
  21.0 105.4 all-reduce.1
Sparse Core Ops, SparseCore 1:
  72.9 45.3 reduce-scatter.1
